TPU v7x, 32 devices: a whole 2x2x4 slice. The times are simulated.
32 devices in a mesh: arc: 2 (over y), trow: 4 (over z), tcol: 4 (over x, core).
Axes of the slice: x: 2, y: 2, z: 4, core: 2. Of those that a mesh axis runs over, the one named last changes fastest.
Arguments:
- design: bfloat16 [1280, 8192], P('arc', 'tcol'), may hold values from -0.25 to 0.25
- local_design: bfloat16 [1280, 128], P('arc'), may hold values from -0.3125 to 0.3125
- lengths: int32 [4], P('arc'), may hold values from 1 to 320, 960 in all
- regularizer: float32 [8192], P(('arc', 'trow')), may hold values from 0.2 to 2
Outputs:
- normal: float32 [8192, 8192], P(('arc', 'trow'), 'tcol')
- panel_factor: float32 [2, 8192, 512], P(None, 'tcol')
Inputs may be any that keep to these rules, and one draw needn't show every extreme that they name: `lengths`: each arc has at least one live row; some arc is full.
All inputs are finite; a program needn't handle non-finite values. No bound on the sum of `lengths` on one device may be relied on, other than what follows from the above.
Results may differ from a plain program's by a relative error of at most 0.003.
Values may be sent and summed in bfloat16 or wider, within the bound.
No kernel may reach another device: no remote copies, remote signals or barrier semaphores. Data moves between devices by JAX's collectives and lax.ppermute only.
A program may use at most 128 MiB of HBM per device.

v0:
```python
import jax
import jax.numpy as jnp
from jax import lax
from jax.sharding import PartitionSpec as P

PANEL = 512
PANELS = 2
ridge = 0.1


def broadcast(block, axis, holder):
    block = jnp.where(lax.axis_index(axis) == holder, block, jnp.zeros_like(block))
    return lax.psum(block, axis)


def project_arcs(design, local_design, lengths):
    arc_count = lengths.shape[0]
    row_count = design.shape[0]
    capacity = row_count // arc_count
    arc_blocks = design.reshape(arc_count, capacity, design.shape[1])
    local_half = local_design.reshape(arc_count, capacity, local_design.shape[1])
    live_rows = jnp.arange(capacity, dtype=jnp.int32)[None, :] < lengths[:, None]
    arc_blocks = jnp.where(live_rows[:, :, None], arc_blocks, jnp.zeros((), design.dtype))
    local_half = jnp.where(live_rows[:, :, None], local_half, jnp.zeros((), local_design.dtype))
    local_normal = jnp.einsum(
        "acl,acm->alm", local_half, local_half, preferred_element_type=jnp.float32
    )
    local_normal = local_normal + ridge * jnp.eye(local_half.shape[2], dtype=jnp.float32)[None]
    local_factor = jnp.linalg.cholesky(local_normal)
    local_cols = local_half.astype(jnp.float32)
    basis_rows = lax.linalg.triangular_solve(
        local_factor, jnp.transpose(local_cols, (0, 2, 1)), left_side=True, lower=True
    )
    basis_rows = basis_rows.astype(jnp.bfloat16)
    loadings = jnp.einsum(
        "alc,acw->alw", basis_rows, arc_blocks, preferred_element_type=jnp.float32
    ).astype(jnp.bfloat16)
    cleaned = arc_blocks.astype(jnp.float32) - jnp.einsum(
        "alc,alw->acw", basis_rows, loadings, preferred_element_type=jnp.float32
    )
    return cleaned.astype(jnp.bfloat16).reshape(row_count, design.shape[1])


def contract_rows(left_rows, right_rows):
    return lax.dot_general(
        left_rows, right_rows, (((0,), (0,)), ((), ())), preferred_element_type=jnp.float32
    )


def per_device(design, local_design, lengths, regularizer):
    row_count, col_width = design.shape
    tile_rows = regularizer.shape[0]
    arc_total = lax.axis_size("arc")
    trow_total = lax.axis_size("trow")
    trow_index = lax.axis_index("trow")
    row_start = (lax.axis_index("arc") * trow_total + trow_index) * tile_rows
    col_start = lax.axis_index("tcol") * col_width
    projected = project_arcs(design, local_design, lengths)
    gathered = lax.all_gather(projected, "tcol", axis=1, tiled=True)
    regrouped = gathered.reshape(row_count, arc_total, trow_total, tile_rows)
    selected = lax.dynamic_slice_in_dim(regrouped, trow_index, 1, 2).reshape(
        row_count, arc_total * tile_rows
    )
    received = lax.all_to_all(selected, "arc", split_axis=1, concat_axis=0, tiled=True)
    normal_block = contract_rows(received, lax.all_gather(projected, "arc", axis=0, tiled=True))
    rows_global = row_start + jnp.arange(tile_rows, dtype=jnp.int32)
    cols_global = col_start + jnp.arange(col_width, dtype=jnp.int32)
    on_diagonal = rows_global[:, None] == cols_global[None, :]
    normal_block = normal_block + jnp.where(
        on_diagonal, regularizer[:, None], jnp.zeros((), jnp.float32)
    )
    panel_factors = []
    for panel_index in range(PANELS):
        lead_col = panel_index * PANEL
        padded_rows = jnp.pad(normal_block, ((PANEL, PANEL), (0, 0)))
        slice_start = jnp.clip(lead_col - row_start + PANEL, 0, tile_rows + PANEL)
        slice_rows = lax.dynamic_slice_in_dim(padded_rows, slice_start, PANEL, 0)
        panel_global = lead_col + jnp.arange(PANEL, dtype=jnp.int32)
        in_tile = (panel_global >= row_start) & (panel_global < row_start + tile_rows)
        own_share = jnp.where(in_tile[:, None], slice_rows, jnp.zeros((), jnp.float32))
        panel_strip = lax.psum(own_share, ("arc", "trow"))
        pivot_block, row_strip = (
            broadcast(panel_strip[:, lead_col : lead_col + PANEL], "tcol", 0),
            broadcast(normal_block[:, lead_col : lead_col + PANEL], "tcol", 0),
        )
        lower_factor = jnp.linalg.cholesky(pivot_block)
        col_factor = lax.linalg.triangular_solve(
            lower_factor, panel_strip, left_side=True, lower=True
        ).T
        row_factor = lax.linalg.triangular_solve(
            lower_factor, row_strip.T, left_side=True, lower=True
        ).T
        col_factor = jnp.where(
            cols_global[:, None] >= lead_col, col_factor, jnp.zeros((), jnp.float32)
        )
        row_factor = jnp.where(
            rows_global[:, None] >= lead_col, row_factor, jnp.zeros((), jnp.float32)
        )
        normal_block = normal_block - jnp.dot(
            row_factor, col_factor.T, precision=lax.Precision.HIGHEST
        )
        panel_factors.append(col_factor)
    return (normal_block, jnp.stack(panel_factors))


def solution(mesh):
    return jax.shard_map(
        per_device,
        mesh=mesh,
        in_specs=(P("arc", "tcol"), P("arc", None), P("arc"), P(("arc", "trow"))),
        out_specs=(P(("arc", "trow"), "tcol"), P(None, "tcol", None)),
        check_vma=False,
    )
```

profile of v0, /device:TPU:0, one launch (start us, length us, event | category | flops | bytes accessed | tf_op | source)
XLA Modules:
  0.0 1101.1 jit_solution(17169129062626182126)
XLA Ops:
  9.6 23.5 %custom-call.33 = f32[2,128,128]{2,1,0:T(8,128)S(1)} custom-call(f32[2,128,128]{2,1,0:T(8,128)S(1)} %fusion.105), custom_call_target="Cholesky" | custom-call | tf_op jit(solution)/shard_map/jit(cholesky)/cholesky | solution.py:29
  33.4 19.7 %custom-call.34 = f32[2,1,128,128]{2,3,1,0:T(8,128)S(1)} custom-call(f32[2,1,128,128]{3,2,1,0:T(8,128)S(1)} %select_bitcast_fusion), custom_call_target="InvertDiagBlocksLowerTriangular" | custom-call | tf_op jit(solution)/shard_map/triangular_solve | solution.py:31
  62.1 72.3 %all-gather.3.cloned.1.call-done = bf16[640,8192]{0,1:T(8,128)(2,1)} async-done(((bf16[640,2048]{0,1:T(8,128)(2,1)}), bf16[640,8192]{0,1:T(8,128)(2,1)}) %all-gather.3.cloned.1.call-update) | async-done | bytes 10485776 | tf_op jit(solution)/shard_map/all_gather | solution.py:59
  143.5 87.0 %all-gather.5.cloned.1.call-done = bf16[1280,2048]{1,0:T(8,128)(2,1)} async-done(((bf16[640,2048]{1,0:T(8,128)(2,1)}), bf16[1280,2048]{1,0:T(8,128)(2,1)}) %all-gather.5.cloned.1.call-update) | async-done | bytes 5242896 | tf_op jit(solution)/shard_map/all_gather | solution.py:65
  248.4 152.4 %all-reduce.10.cloned.1.call-done = f32[512,2048]{0,1:T(8,128)} async-done(((f32[512,2048]{0,1:T(8,128)}), f32[512,2048]{0,1:T(8,128)}) %all-reduce.10.cloned.1.call-update) | async-done | bytes 4194320 | tf_op jit(solution)/shard_map/psum | solution.py:81
  403.2 67.9 %all-reduce.16.cloned.1.call-done = (f32[512,512]{0,1:T(8,128)}, f32[512,1024]{1,0:T(8,128)}) async-done(((f32[512,512]{0,1:T(8,128)}, f32[512,1024]{1,0:T(8,128)}), (f32[512,512]{0,1:T(8,128)}, f32[512,1024]{1,0:T(8,128)})) %all-reduce.16.cloned.1.call-update) | async-done | bytes 3145744 | tf_op jit(solution)/shard_map/psum | solution.py:13
  474.1 11.7 %cholesky.327 = f32[128,128]{1,0:T(8,128)S(1)} custom-call(f32[128,128]{1,0:T(8,128)S(1)} %cholesky.467), custom_call_target="Cholesky" | custom-call | tf_op jit(solution)/shard_map/jit(cholesky)/cholesky | solution.py:86
  496.5 11.7 %cholesky.346 = f32[128,128]{1,0:T(8,128)S(1)} custom-call(f32[128,128]{1,0:T(8,128)S(1)} %cholesky.471), custom_call_target="Cholesky" | custom-call | tf_op jit(solution)/shard_map/jit(cholesky)/cholesky | solution.py:86
  508.2 10.0 custom-call.41
  518.8 11.7 %cholesky.367 = f32[128,128]{1,0:T(8,128)S(1)} custom-call(f32[128,128]{1,0:T(8,128)S(1)} %cholesky.476), custom_call_target="Cholesky" | custom-call | tf_op jit(solution)/shard_map/jit(cholesky)/cholesky | solution.py:86
  530.6 9.8 custom-call.42
  541.0 11.7 %cholesky.384 = f32[128,128]{1,0:T(8,128)S(1)} custom-call(f32[128,128]{1,0:T(8,128)S(1)} %convolution_subtract_fusion.15), custom_call_target="Cholesky" | custom-call | tf_op jit(solution)/shard_map/jit(cholesky)/cholesky | solution.py:86
  566.2 39.3 %custom-call.43 = f32[4,128,128]{1,2,0:T(8,128)S(1)} custom-call(f32[4,128,128]{2,1,0:T(8,128)S(1)} %get-tuple-element.33), custom_call_target="InvertDiagBlocksLowerTriangular" | custom-call | tf_op jit(solution)/shard_map/triangular_solve/custom-call.9 | solution.py:90
  639.3 15.1 %convolution_subtract_fusion.1 = f32[1024,2048]{0,1:T(8,128)S(1)} fusion(f32[1024,2048]{0,1:T(8,128)S(1)} %bitcast.164, f32[128,2048]{0,1:T(8,128)S(1)} %fusion.128, f32[128,2048]{0,1:T(8,128)S(1)} %copy-done.4, f32[128,2048]{0,1:T(8,128)S(1)} %copy-done.3, f32[128,2048]{0,1:T(8,128)S(1)} %copy.71, f32[128,1024]{1,0:T(8,128)S(1)} %fusion.129, ...), kind=kOutput, calls=%fused_computation.14 | convolution fusion | flops 12893290496 | bytes 23071744 | tf_op jit(solution)/shard_map/dot_general | solution.py:99
  664.2 153.4 %all-reduce.12.cloned.1.call-done = f32[512,2048]{0,1:T(8,128)} async-done(((f32[512,2048]{0,1:T(8,128)}), f32[512,2048]{0,1:T(8,128)}) %all-reduce.12.cloned.1.call-update) | async-done | bytes 4194320 | tf_op jit(solution)/shard_map/psum | solution.py:81
  823.6 64.4 %all-reduce.14.cloned.1.call-done = (f32[512,512]{0,1:T(8,128)}, f32[512,1024]{1,0:T(8,128)}) async-done(((f32[512,512]{0,1:T(8,128)}, f32[512,1024]{1,0:T(8,128)}), (f32[512,512]{0,1:T(8,128)}, f32[512,1024]{1,0:T(8,128)})) %all-reduce.14.cloned.1.call-update) | async-done | bytes 3145744 | tf_op jit(solution)/shard_map/psum | solution.py:13
  891.0 11.7 %cholesky.399 = f32[128,128]{1,0:T(8,128)S(1)} custom-call(f32[128,128]{1,0:T(8,128)S(1)} %cholesky.480), custom_call_target="Cholesky" | custom-call | tf_op jit(solution)/shard_map/jit(cholesky)/cholesky | solution.py:86
  913.4 11.7 %cholesky.418 = f32[128,128]{1,0:T(8,128)S(1)} custom-call(f32[128,128]{1,0:T(8,128)S(1)} %cholesky.484), custom_call_target="Cholesky" | custom-call | tf_op jit(solution)/shard_map/jit(cholesky)/cholesky | solution.py:86
  925.1 10.0 custom-call.46
  935.8 11.7 %cholesky.439 = f32[128,128]{1,0:T(8,128)S(1)} custom-call(f32[128,128]{1,0:T(8,128)S(1)} %cholesky.489), custom_call_target="Cholesky" | custom-call | tf_op jit(solution)/shard_map/jit(cholesky)/cholesky | solution.py:86
  947.5 9.8 custom-call.47
  957.9 11.7 %cholesky.456 = f32[128,128]{1,0:T(8,128)S(1)} custom-call(f32[128,128]{1,0:T(8,128)S(1)} %convolution_subtract_fusion.14), custom_call_target="Cholesky" | custom-call | tf_op jit(solution)/shard_map/jit(cholesky)/cholesky | solution.py:86
  983.6 39.3 %custom-call.48 = f32[4,128,128]{1,2,0:T(8,128)S(1)} custom-call(f32[4,128,128]{2,1,0:T(8,128)S(1)} %get-tuple-element.35), custom_call_target="InvertDiagBlocksLowerTriangular" | custom-call | tf_op jit(solution)/shard_map/triangular_solve/custom-call.9 | solution.py:90
  1060.6 16.5 %convolution_subtract_fusion = f32[1024,2048]{0,1:T(8,128)} fusion(f32[1024,2048]{0,1:T(8,128)S(1)} %bitcast.162, f32[128,2048]{0,1:T(8,128)S(1)} %fusion.134, f32[128,2048]{0,1:T(8,128)S(1)} %copy-done.7, f32[128,2048]{0,1:T(8,128)S(1)} %copy-done.6, f32[128,2048]{0,1:T(8,128)S(1)} %copy.80, f32[128,1024]{1,0:T(8,128)S(1)} %fusion.135, ...), kind=kOutput, calls=%fused_computation.13 | convolution fusion | flops 12893290496 | bytes 23071744 | tf_op jit(solution)/shard_map/dot_general | solution.py:99
  (192 shorter events, 212.8 us)
Async XLA Ops:
  7.2 127.3 %all-gather.3.cloned.1.call-start = ((), (), s32[]{:S(2)}) async-start(), calls=%async_computation.1 | async-start | bytes 13107200 | tf_op jit(solution)/shard_map/all_gather | solution.py:59
  58.4 3.1 copy-start.2
  61.4 169.1 %all-gather.5.cloned.1.call-start = ((), (), s32[]{:S(2)}) async-start(), calls=%async_computation.2 | async-start | bytes 7864320 | tf_op jit(solution)/shard_map/all_gather | solution.py:65
  136.4 94.1 %copy-start.12 = (f32[1024]{0:T(1024)S(1)}, f32[1024]{0:T(1024)}, u32[]{:S(2)}) copy-start(f32[1024]{0:T(1024)} %param.12) | copy-start | bytes 12292
  139.0 91.4 %all-to-all-start = ((bf16[640,2,1024]{2,0,1:T(8,128)(2,1)}), bf16[640,2,1024]{2,0,1:T(8,128)(2,1)S(1)}, u32[]{:S(2)}, u32[]{:S(2)}) async-start(bf16[640,2,1024]{2,0,1:T(8,128)(2,1)} %bitcast.7), calls=%async_computation | async-start | bytes 5242880 | tf_op jit(solution)/shard_map/all_to_all | solution.py:64
  142.9 257.8 %all-reduce.10.cloned.1.call-start = ((), (), s32[]{:S(2)}) async-start(), calls=%async_computation.3 | async-start | bytes 8388608 | tf_op jit(solution)/shard_map/psum | solution.py:81
  238.5 3.4 copy-start.1
  245.1 226.0 %all-reduce.16.cloned.1.call-start = ((), (), s32[]{:S(2)}) async-start(), calls=%async_computation.6 | async-start | bytes 6291456 | tf_op jit(solution)/shard_map/psum | solution.py:13
  403.0 414.6 %all-reduce.12.cloned.1.call-start = ((), (), s32[]{:S(2)}) async-start(), calls=%async_computation.4 | async-start | bytes 8388608 | tf_op jit(solution)/shard_map/psum | solution.py:81
  566.2 42.0 %copy-start.9 = (f32[512,512]{1,0:T(8,128)}, f32[512,512]{1,0:T(8,128)S(1)}, u32[]{:S(2)}) copy-start(f32[512,512]{1,0:T(8,128)S(1)} %get-tuple-element.210) | copy-start | bytes 3145732
  623.1 8.3 copy-start.10
  623.1 16.2 %slice-start.2 = ((s8[8388608]{0:T(1024)(128)(4,1)}), s8[4194304]{0:T(1024)(128)(4,1)S(1)}, s32[]{:S(2)}) async-start(s8[8388608]{0:T(1024)(128)(4,1)} %bitcast.163), calls=%async_computation.9 | async-start | bytes 8388608
  631.4 7.9 copy-start.5
  632.1 7.2 slice-start.3
  633.7 5.7 copy-start.3
  633.7 5.7 copy-start.4
  654.4 3.4 copy-start
  661.0 227.0 %all-reduce.14.cloned.1.call-start = ((), (), s32[]{:S(2)}) async-start(), calls=%async_computation.5 | async-start | bytes 6291456 | tf_op jit(solution)/shard_map/psum | solution.py:13
  983.6 42.0 %copy-start.8 = (f32[512,512]{1,0:T(8,128)}, f32[512,512]{1,0:T(8,128)S(1)}, u32[]{:S(2)}) copy-start(f32[512,512]{1,0:T(8,128)S(1)} %get-tuple-element.209) | copy-start | bytes 3145732
  1040.5 8.6 copy-start.11
  1051.1 5.8 copy-start.6
  1051.1 5.8 copy-start.7
  1051.7 7.5 slice-start
  1056.9 3.7 slice-start.1
Sparse Core Ops, SparseCore 0:
  61.5 72.8 all-gather.2
  136.5 93.8 all-gather.4
  245.2 155.4 all-reduce.9
  403.6 67.4 all-reduce.15
  661.1 156.4 all-reduce.11
  820.5 67.4 all-reduce.13
where the time goes:
time: 1110 us; the launch traced here: 1100 us
  waiting for transfers between devices  598 us (54%)
  other arithmetic  316 us (28%)
  matrix products  109 us (10%)
  local copies, waits for them, and re-layouts  52.6 us (5%)
  between operations  20.3 us (2%)
    psum x2, waiting for transfers between devices, per_device(): panel_strip = lax.psum(own_share, ('arc', 'trow'))  306 us
    another operation x30, other arithmetic, per_device(): lower_factor = jnp.linalg.cholesky(pivot_block)  158 us
    psum x2, waiting for transfers between devices, broadcast(): return lax.psum(block, axis)  132 us
    all_gather x1, waiting for transfers between devices, per_device(): lax.all_gather(projected, 'arc', axis=0, tiled=True)  87 us
    another operation x5, other arithmetic, per_device(): lax.linalg.triangular_solve(lower_factor, row_strip.T, left_side=True, lo...  79.5 us
    all_gather x1, waiting for transfers between devices, per_device(): gathered = lax.all_gather(projected, 'tcol', axis=1, tiled=True)  72.3 us
    another operation x14, matrix products, per_device(): lax.linalg.triangular_solve(lower_factor, panel_strip, left_side=True, lo...  43.5 us
    dot_general x2, matrix products, per_device(): jnp.dot(row_factor, col_factor.T, precision=lax.Precision.HIGHEST)  31.6 us
  transfers between devices with their start and end apart: 7, of which 6 were waited for; matrix products, arithmetic and copies ran while one was open for 1% of the time, Pallas kernels for 0%

commit v1 on v0

--- a/solution.py
+++ b/solution.py
@@ -78,7 +78,7 @@
         panel_global = lead_col + jnp.arange(PANEL, dtype=jnp.int32)
         in_tile = (panel_global >= row_start) & (panel_global < row_start + tile_rows)
         own_share = jnp.where(in_tile[:, None], slice_rows, jnp.zeros((), jnp.float32))
-        panel_strip = lax.psum(own_share, ("arc", "trow"))
+        panel_strip = lax.psum(lax.psum(own_share, axis_name="trow"), axis_name="arc")
         pivot_block, row_strip = (
             broadcast(panel_strip[:, lead_col : lead_col + PANEL], "tcol", 0),
             broadcast(normal_block[:, lead_col : lead_col + PANEL], "tcol", 0),

time: 1110 us -> 1330 us (1.20)
  waiting for transfers between devices: 598 us -> 816 us
    psum x2 -> x4, waiting for transfers between devices: 306 us -> 521 us  [the longest x2 309 us: per_device(): lax.psum(own_share, axis_name='trow')]
  transfers between devices with their start and end apart: 7 -> 9, of which waited for: 6 -> 8; matrix products, arithmetic and copies ran while one was open for 1% -> 1% of each run, Pallas kernels for 0% -> 0%
where the time goes in v1:
time: 1330 us; the launch traced here: 1320 us
  waiting for transfers between devices  816 us (61%)
  other arithmetic  316 us (24%)
  matrix products  109 us (8%)
  local copies, waits for them, and re-layouts  52.6 us (4%)
  between operations  20.3 us (2%)
    psum x2, waiting for transfers between devices, per_device(): lax.psum(own_share, axis_name='trow')  309 us
    psum x2, waiting for transfers between devices, per_device(): lax.psum(lax.psum(own_share, axis_name='trow'), axis_name='arc')  212 us
    another operation x30, other arithmetic, per_device(): lower_factor = jnp.linalg.cholesky(pivot_block)  158 us
    psum x2, waiting for transfers between devices, broadcast(): return lax.psum(block, axis)  134 us
    all_gather x1, waiting for transfers between devices, per_device(): lax.all_gather(projected, 'arc', axis=0, tiled=True)  87 us
    another operation x5, other arithmetic, per_device(): lax.linalg.triangular_solve(lower_factor, row_strip.T, left_side=True, lo...  79.5 us
    all_gather x1, waiting for transfers between devices, per_device(): gathered = lax.all_gather(projected, 'tcol', axis=1, tiled=True)  72.3 us
    another operation x14, matrix products, per_device(): lax.linalg.triangular_solve(lower_factor, panel_strip, left_side=True, lo...  43.5 us
  transfers between devices with their start and end apart: 9, of which 8 were waited for; matrix products, arithmetic and copies ran while one was open for 1% of the time, Pallas kernels for 0%

profile of v1, /device:TPU:0, one launch (start us, length us, event | category | flops | bytes accessed | tf_op | source)
XLA Modules:
  0.0 1319.0 jit_solution(3691318049182748165)
XLA Ops:
  9.6 23.5 %custom-call.33 = f32[2,128,128]{2,1,0:T(8,128)S(1)} custom-call(f32[2,128,128]{2,1,0:T(8,128)S(1)} %fusion.105), custom_call_target="Cholesky" | custom-call | tf_op jit(solution)/shard_map/jit(cholesky)/cholesky | solution.py:29
  33.4 19.7 %custom-call.34 = f32[2,1,128,128]{2,3,1,0:T(8,128)S(1)} custom-call(f32[2,1,128,128]{3,2,1,0:T(8,128)S(1)} %select_bitcast_fusion), custom_call_target="InvertDiagBlocksLowerTriangular" | custom-call | tf_op jit(solution)/shard_map/triangular_solve | solution.py:31
  62.1 72.3 %all-gather.3.cloned.1.call-done = bf16[640,8192]{0,1:T(8,128)(2,1)} async-done(((bf16[640,2048]{0,1:T(8,128)(2,1)}), bf16[640,8192]{0,1:T(8,128)(2,1)}) %all-gather.3.cloned.1.call-update) | async-done | bytes 10485776 | tf_op jit(solution)/shard_map/all_gather | solution.py:59
  143.5 87.0 %all-gather.5.cloned.1.call-done = bf16[1280,2048]{1,0:T(8,128)(2,1)} async-done(((bf16[640,2048]{1,0:T(8,128)(2,1)}), bf16[1280,2048]{1,0:T(8,128)(2,1)}) %all-gather.5.cloned.1.call-update) | async-done | bytes 5242896 | tf_op jit(solution)/shard_map/all_gather | solution.py:65
  245.1 154.2 %all-reduce.12.cloned.1.call-done = f32[512,2048]{0,1:T(8,128)} async-done(((f32[512,2048]{0,1:T(8,128)}), f32[512,2048]{0,1:T(8,128)}) %all-reduce.12.cloned.1.call-update) | async-done | bytes 4194320 | tf_op jit(solution)/shard_map/psum | solution.py:81
  402.6 105.9 %all-reduce.14.cloned.1.call-done = f32[512,2048]{0,1:T(8,128)} async-done(((f32[512,2048]{0,1:T(8,128)}), f32[512,2048]{0,1:T(8,128)}) %all-reduce.14.cloned.1.call-update) | async-done | bytes 4194320 | tf_op jit(solution)/shard_map/psum | solution.py:81
  511.0 68.9 %all-reduce.22.cloned.1.call-done = (f32[512,512]{0,1:T(8,128)}, f32[512,1024]{1,0:T(8,128)}) async-done(((f32[512,512]{0,1:T(8,128)}, f32[512,1024]{1,0:T(8,128)}), (f32[512,512]{0,1:T(8,128)}, f32[512,1024]{1,0:T(8,128)})) %all-reduce.22.cloned.1.call-update) | async-done | bytes 3145744 | tf_op jit(solution)/shard_map/psum | solution.py:13
  582.9 11.7 cholesky.327
  605.3 11.7 cholesky.346
  617.0 10.0 custom-call.41
  627.6 11.7 cholesky.367
  649.8 11.7 cholesky.384
  675.0 39.3 %custom-call.43 = f32[4,128,128]{1,2,0:T(8,128)S(1)} custom-call(f32[4,128,128]{2,1,0:T(8,128)S(1)} %get-tuple-element.33), custom_call_target="InvertDiagBlocksLowerTriangular" | custom-call | tf_op jit(solution)/shard_map/triangular_solve/custom-call.9 | solution.py:90
  748.1 15.1 %convolution_subtract_fusion.1 = f32[1024,2048]{0,1:T(8,128)S(1)} fusion(f32[1024,2048]{0,1:T(8,128)S(1)} %bitcast.164, f32[128,2048]{0,1:T(8,128)S(1)} %fusion.128, f32[128,2048]{0,1:T(8,128)S(1)} %copy-done.4, f32[128,2048]{0,1:T(8,128)S(1)} %copy-done.3, f32[128,2048]{0,1:T(8,128)S(1)} %copy.71, f32[128,1024]{1,0:T(8,128)S(1)} %fusion.129, ...), kind=kOutput, calls=%fused_computation.14 | convolution fusion | flops 12893290496 | bytes 23071744 | tf_op jit(solution)/shard_map/dot_general | solution.py:99
  769.9 155.2 %all-reduce.16.cloned.1.call-done = f32[512,2048]{0,1:T(8,128)} async-done(((f32[512,2048]{0,1:T(8,128)}), f32[512,2048]{0,1:T(8,128)}) %all-reduce.16.cloned.1.call-update) | async-done | bytes 4194320 | tf_op jit(solution)/shard_map/psum | solution.py:81
  928.3 106.1 %all-reduce.18.cloned.1.call-done = f32[512,2048]{0,1:T(8,128)} async-done(((f32[512,2048]{0,1:T(8,128)}), f32[512,2048]{0,1:T(8,128)}) %all-reduce.18.cloned.1.call-update) | async-done | bytes 4194320 | tf_op jit(solution)/shard_map/psum | solution.py:81
  1040.4 65.5 %all-reduce.20.cloned.1.call-done = (f32[512,512]{0,1:T(8,128)}, f32[512,1024]{1,0:T(8,128)}) async-done(((f32[512,512]{0,1:T(8,128)}, f32[512,1024]{1,0:T(8,128)}), (f32[512,512]{0,1:T(8,128)}, f32[512,1024]{1,0:T(8,128)})) %all-reduce.20.cloned.1.call-update) | async-done | bytes 3145744 | tf_op jit(solution)/shard_map/psum | solution.py:13
  1108.9 11.7 cholesky.399
  1131.3 11.7 cholesky.418
  1143.1 10.0 custom-call.46
  1153.7 11.7 cholesky.439
  1175.9 11.7 cholesky.456
  1201.5 39.3 %custom-call.48 = f32[4,128,128]{1,2,0:T(8,128)S(1)} custom-call(f32[4,128,128]{2,1,0:T(8,128)S(1)} %get-tuple-element.35), custom_call_target="InvertDiagBlocksLowerTriangular" | custom-call | tf_op jit(solution)/shard_map/triangular_solve/custom-call.9 | solution.py:90
  1278.5 16.5 %convolution_subtract_fusion = f32[1024,2048]{0,1:T(8,128)} fusion(f32[1024,2048]{0,1:T(8,128)S(1)} %bitcast.162, f32[128,2048]{0,1:T(8,128)S(1)} %fusion.134, f32[128,2048]{0,1:T(8,128)S(1)} %copy-done.7, f32[128,2048]{0,1:T(8,128)S(1)} %copy-done.6, f32[128,2048]{0,1:T(8,128)S(1)} %copy.80, f32[128,1024]{1,0:T(8,128)S(1)} %fusion.135, ...), kind=kOutput, calls=%fused_computation.13 | convolution fusion | flops 12893290496 | bytes 23071744 | tf_op jit(solution)/shard_map/dot_general | solution.py:99
  (198 shorter events, 232.6 us)
Async XLA Ops:
  7.2 127.3 %all-gather.3.cloned.1.call-start = ((), (), s32[]{:S(2)}) async-start(), calls=%async_computation.1 | async-start | bytes 13107200 | tf_op jit(solution)/shard_map/all_gather | solution.py:59
  61.4 169.1 %all-gather.5.cloned.1.call-start = ((), (), s32[]{:S(2)}) async-start(), calls=%async_computation.2 | async-start | bytes 7864320 | tf_op jit(solution)/shard_map/all_gather | solution.py:65
  136.4 94.1 %copy-start.12 = (f32[1024]{0:T(1024)S(1)}, f32[1024]{0:T(1024)}, u32[]{:S(2)}) copy-start(f32[1024]{0:T(1024)} %param.12) | copy-start | bytes 12292
  139.0 91.4 %all-to-all-start = ((bf16[640,2,1024]{2,0,1:T(8,128)(2,1)}), bf16[640,2,1024]{2,0,1:T(8,128)(2,1)S(1)}, u32[]{:S(2)}, u32[]{:S(2)}) async-start(bf16[640,2,1024]{2,0,1:T(8,128)(2,1)} %bitcast.7), calls=%async_computation | async-start | bytes 5242880 | tf_op jit(solution)/shard_map/all_to_all | solution.py:64
  142.9 256.4 %all-reduce.12.cloned.1.call-start = ((), (), s32[]{:S(2)}) async-start(), calls=%async_computation.3 | async-start | bytes 8388608 | tf_op jit(solution)/shard_map/psum | solution.py:81
  238.5 3.4 copy-start.1
  245.1 263.4 %all-reduce.14.cloned.1.call-start = ((), (), s32[]{:S(2)}) async-start(), calls=%async_computation.4 | async-start | bytes 8388608 | tf_op jit(solution)/shard_map/psum | solution.py:81
  399.4 180.5 %all-reduce.22.cloned.1.call-start = ((), (), s32[]{:S(2)}) async-start(), calls=%async_computation.8 | async-start | bytes 6291456 | tf_op jit(solution)/shard_map/psum | solution.py:13
  510.9 414.2 %all-reduce.16.cloned.1.call-start = ((), (), s32[]{:S(2)}) async-start(), calls=%async_computation.5 | async-start | bytes 8388608 | tf_op jit(solution)/shard_map/psum | solution.py:81
  675.0 42.0 %copy-start.9 = (f32[512,512]{1,0:T(8,128)}, f32[512,512]{1,0:T(8,128)S(1)}, u32[]{:S(2)}) copy-start(f32[512,512]{1,0:T(8,128)S(1)} %get-tuple-element.212) | copy-start | bytes 3145732
  731.9 8.3 copy-start.10
  731.9 16.2 %slice-start.2 = ((s8[8388608]{0:T(1024)(128)(4,1)}), s8[4194304]{0:T(1024)(128)(4,1)S(1)}, s32[]{:S(2)}) async-start(s8[8388608]{0:T(1024)(128)(4,1)} %bitcast.163), calls=%async_computation.11 | async-start | bytes 8388608
  740.2 7.9 copy-start.5
  740.9 7.2 slice-start.3
  742.5 5.7 copy-start.3
  742.5 5.7 copy-start.4
  769.8 264.6 %all-reduce.18.cloned.1.call-start = ((), (), s32[]{:S(2)}) async-start(), calls=%async_computation.6 | async-start | bytes 8388608 | tf_op jit(solution)/shard_map/psum | solution.py:81
  925.1 180.8 %all-reduce.20.cloned.1.call-start = ((), (), s32[]{:S(2)}) async-start(), calls=%async_computation.7 | async-start | bytes 6291456 | tf_op jit(solution)/shard_map/psum | solution.py:13
  1201.5 42.0 %copy-start.8 = (f32[512,512]{1,0:T(8,128)}, f32[512,512]{1,0:T(8,128)S(1)}, u32[]{:S(2)}) copy-start(f32[512,512]{1,0:T(8,128)S(1)} %get-tuple-element.211) | copy-start | bytes 3145732
  1258.4 8.6 copy-start.11
  1269.0 5.8 copy-start.6
  1269.0 5.8 copy-start.7
  1269.7 7.5 slice-start
  1274.8 3.7 slice-start.1
  (2 other events, 6.5 us)
Sparse Core Ops, SparseCore 0:
  61.5 72.8 all-gather.2
  136.5 93.8 all-gather.4
  245.2 154.0 all-reduce.11
  401.6 106.8 all-reduce.13
  511.4 68.4 all-reduce.21
  769.9 155.0 all-reduce.15
  927.5 106.8 all-reduce.17
  1037.4 68.4 all-reduce.19
